TPU v7x, 256 devices: a whole 4x4x8 slice. The times are simulated.
256 devices in a mesh: dp: 4 (over x), state: 64 (over y, z, core).
Axes of the slice: x: 4, y: 4, z: 8, core: 2. Of those that a mesh axis runs over, the one named last changes fastest.
Arguments:
- alpha_init: bfloat16 [32, 1024, 1024], P('dp', 'state'), may hold values from 0.099609375 to 4
- tokens: int32 [32, 3], P('dp'), may hold values from 0 to 511
- trans_rows: bfloat16 [1024, 1024], replicated, may hold values from 5e-05 to 1.11, as said below
- trans_cols: bfloat16 [1024, 1024], replicated, may hold values from 5e-05 to 1.11, as said below
- emit_rows: bfloat16 [512, 1024], replicated, may hold values from 0.001 to 1, as said below
- emit_cols: bfloat16 [512, 1024], replicated, may hold values from 0.001 to 1, as said below
- backward: bfloat16 [3, 32, 1024, 1024], P(None, 'dp', None, 'state'), may hold values from 0.2 to 32, as said below
Outputs:
- alpha_final: bfloat16 [32, 1024, 1024], P('dp', 'state')
- counts_rows: float32 [1024, 1024], P(None, ('dp', 'state'))
- counts_cols: float32 [1024, 1024], P(None, ('dp', 'state'))
- loglik: float32 [32], P('dp')
Inputs may be any that keep to these rules, and one draw needn't show every extreme that they name: `trans_rows`: positive transition weights. `trans_cols`: positive transition weights. `emit_rows`: positive emission weights. `emit_cols`: positive emission weights. Positive backward weights.
All inputs are finite; a program needn't handle non-finite values.
Results may differ from a plain program's by a relative error of at most 0.0046.
Values may be sent and summed in bfloat16 or wider, within the bound.
No kernel may reach another device: no remote copies, remote signals or barrier semaphores. Data moves between devices by JAX's collectives and lax.ppermute only.
A program may use at most 128 MiB of HBM per device.

v0:
```python
import jax
import jax.numpy as jnp
from jax import lax
from jax.sharding import PartitionSpec as P

STEPS = 3


def on_device(alpha_init, tokens, trans_rows, trans_cols, emit_rows, emit_cols, backward):
    f32 = jnp.float32
    groups = lax.axis_size("state")
    seq_dev = alpha_init.shape[0]
    width_rows = trans_rows.shape[0]
    width_cols = trans_cols.shape[0]
    cols_dev = width_cols // groups
    offset = lax.axis_index("state") * cols_dev
    alpha = alpha_init
    sums_rows = jnp.zeros((width_rows, width_rows), f32)
    sums_cols = jnp.zeros((width_cols, width_cols), f32)
    loglik = jnp.zeros((seq_dev,), f32)
    for step in range(STEPS):
        tok = tokens[:, step]
        first = jnp.take(emit_rows, tok, axis=0).astype(f32)
        second_all = jnp.take(emit_cols, tok, axis=0)
        second = lax.dynamic_slice_in_dim(second_all, offset, cols_dev, 1).astype(f32)
        mixed = jnp.einsum("sij,jk->sik", alpha, trans_cols, preferred_element_type=f32).astype(
            jnp.bfloat16
        )
        mixed_cols = lax.all_to_all(mixed, "state", split_axis=2, concat_axis=1, tiled=True)
        moved = jnp.einsum("sik,il->slk", mixed_cols, trans_rows, preferred_element_type=f32)
        emission = first[:, :, None] * second[:, None, :]
        scaled = moved * emission
        total = lax.psum(jnp.sum(scaled, axis=(1, 2)), "state")
        norm = total / (width_rows * width_cols)
        weight = (emission * backward[step].astype(f32) / norm[:, None, None]).astype(jnp.bfloat16)
        pulled = jnp.einsum("il,slk->sik", trans_rows, weight, preferred_element_type=f32).astype(
            jnp.bfloat16
        )
        pulled_local = lax.all_to_all(pulled, "state", split_axis=1, concat_axis=2, tiled=True)
        sums_rows = sums_rows + jnp.einsum(
            "sik,slk->il", mixed_cols, weight, preferred_element_type=f32
        )
        sums_cols = sums_cols + jnp.einsum(
            "sij,sik->jk", alpha, pulled_local, preferred_element_type=f32
        )
        loglik = loglik + jnp.log(norm)
        fresh = (scaled / norm[:, None, None]).astype(jnp.bfloat16)
        alpha = lax.all_to_all(fresh, "state", split_axis=1, concat_axis=2, tiled=True)
    factor = 1.0 / (seq_dev * lax.axis_size("dp") * STEPS)
    terms_rows = trans_rows.astype(f32) * sums_rows * factor
    terms_cols = trans_cols.astype(f32) * sums_cols * factor
    counts_rows, counts_cols = (
        lax.psum_scatter(terms_rows, ("dp", "state"), scatter_dimension=1, tiled=True),
        lax.psum_scatter(terms_cols, ("dp", "state"), scatter_dimension=1, tiled=True),
    )
    return (alpha, counts_rows, counts_cols, loglik)


def solution(mesh):
    return jax.shard_map(
        on_device,
        mesh=mesh,
        in_specs=(
            P("dp", "state", None),
            P("dp", None),
            P(),
            P(),
            P(),
            P(),
            P(None, "dp", None, "state"),
        ),
        out_specs=(
            P("dp", "state", None),
            P(None, ("dp", "state")),
            P(None, ("dp", "state")),
            P("dp"),
        ),
        check_vma=False,
    )
```

profile of v0, /device:TPU:2, one launch (start us, length us, event | category | flops | bytes accessed | tf_op | source)
XLA Modules:
  0.0 962.1 jit_solution(3449522075632876979)
XLA Ops:
  14.0 12.1 %all-to-all-start = ((bf16[64,2,1024]{2,1,0:T(2,128)(2,1)}), bf16[64,2,1024]{2,1,0:T(2,128)(2,1)S(1)}, u32[]{:S(2)}, u32[]{:S(2)}) async-start(bf16[64,2,1024]{2,1,0:T(2,128)(2,1)} %reshape.105), calls=%async_computation | async-start | bytes 524288 | tf_op jit(solution)/shard_map/all_to_all | solution.py:29
  28.8 9.3 all-to-all-done
  42.2 4.8 all_to_all.120
  48.3 125.5 %psum.21 = f32[8]{0:T(128)S(1)} all-reduce(f32[8]{0:T(128)S(1)} %get-tuple-element.19), channel_id=1, replica_groups=mesh['dp'=4,'state'=64] {'state'}, use_global_device_ids=true, to_apply=%region_1.3 | all-reduce | flops 8 | bytes 64 | tf_op jit(solution)/shard_map/psum | solution.py:33
  181.1 6.0 all-to-all-start.1
  190.4 8.6 all-to-all-done.1
  204.5 4.8 all_to_all.124
  216.6 6.0 all-to-all-start.2
  240.7 10.6 %all-to-all-start.6 = ((bf16[64,2,1024]{2,1,0:T(2,128)(2,1)}), bf16[64,2,1024]{2,1,0:T(2,128)(2,1)}, u32[]{:S(2)}, u32[]{:S(2)}) async-start(bf16[64,2,1024]{2,1,0:T(2,128)(2,1)} %reshape.117), calls=%async_computation.6 | async-start | bytes 524288 | tf_op jit(solution)/shard_map/all_to_all | solution.py:39
  264.8 128.9 %psum.22 = f32[8]{0:T(128)S(1)} all-reduce(f32[8]{0:T(128)S(1)} %get-tuple-element.21), channel_id=1, replica_groups=mesh['dp'=4,'state'=64] {'state'}, use_global_device_ids=true, to_apply=%region_3.5 | all-reduce | flops 8 | bytes 64 | tf_op jit(solution)/shard_map/psum | solution.py:33
  402.3 4.8 all-to-all-start.3
  418.8 5.3 all_to_all.144
  433.5 10.7 %all-to-all-start.7 = ((bf16[64,2,1024]{2,1,0:T(2,128)(2,1)}), bf16[64,2,1024]{2,1,0:T(2,128)(2,1)S(1)}, u32[]{:S(2)}, u32[]{:S(2)}) async-start(bf16[64,2,1024]{2,1,0:T(2,128)(2,1)} %reshape.119), calls=%async_computation.7 | async-start | bytes 524288 | tf_op jit(solution)/shard_map/all_to_all | solution.py:39
  464.3 10.9 %all-to-all-start.4 = ((bf16[64,2,1024]{2,1,0:T(2,128)(2,1)}), bf16[64,2,1024]{2,1,0:T(2,128)(2,1)S(1)}, u32[]{:S(2)}, u32[]{:S(2)}) async-start(bf16[64,2,1024]{2,1,0:T(2,128)(2,1)} %reshape.113), calls=%async_computation.4 | async-start | bytes 524288 | tf_op jit(solution)/shard_map/all_to_all | solution.py:29
  494.7 4.8 all_to_all.136
  500.8 129.1 %psum.23 = f32[8]{0:T(128)S(1)} all-reduce(f32[8]{0:T(128)S(1)} %get-tuple-element.23), channel_id=1, replica_groups=mesh['dp'=4,'state'=64] {'state'}, use_global_device_ids=true, to_apply=%region_5.7 | all-reduce | flops 8 | bytes 64 | tf_op jit(solution)/shard_map/psum | solution.py:33
  643.9 6.5 fusion.4
  650.4 5.4 all-to-all-done.8
  660.0 4.8 all_to_all.152
  664.8 6.4 fusion.2
  677.0 6.3 all-to-all-start.5
  683.2 13.2 %all-to-all-done.5 = bf16[64,2,1024]{2,1,0:T(2,128)(2,1)S(1)} async-done(((bf16[64,2,1024]{2,1,0:T(2,128)(2,1)}), bf16[64,2,1024]{2,1,0:T(2,128)(2,1)S(1)}, u32[]{:S(2)}, u32[]{:S(2)}) %all-to-all-start.5) | async-done | bytes 262176 | tf_op jit(solution)/shard_map/all_to_all | solution.py:48
  700.6 5.4 all_to_all.140
  706.0 246.3 %all-reduce.5.cloned.1.call-done = (f32[1024,1024]{0,1:T(8,128)}, f32[1024,1024]{0,1:T(8,128)}) async-done(((f32[1024,1024]{0,1:T(8,128)}, f32[1024,1024]{0,1:T(8,128)}), (f32[1024,1024]{0,1:T(8,128)}, f32[1024,1024]{0,1:T(8,128)})) %all-reduce.5.cloned.1.call-update) | async-done | bytes 8388624
  (105 shorter events, 170.7 us)
Async XLA Ops:
  7.2 20.9 %copy-start = (bf16[512,1024]{1,0:T(8,128)(2,1)S(1)}, bf16[512,1024]{1,0:T(8,128)(2,1)}, u32[]{:S(2)}) copy-start(bf16[512,1024]{1,0:T(8,128)(2,1)} %param.13) | copy-start | bytes 3145732
  9.4 16.7 %copy-start.9 = (s32[8,3]{0,1:T(4,128)S(1)}, s32[8,3]{0,1:T(4,128)}, u32[]{:S(2)}) copy-start(s32[8,3]{0,1:T(4,128)} %param.10) | copy-start | bytes 292
  14.0 24.1 %all-to-all-start = ((bf16[64,2,1024]{2,1,0:T(2,128)(2,1)}), bf16[64,2,1024]{2,1,0:T(2,128)(2,1)S(1)}, u32[]{:S(2)}, u32[]{:S(2)}) async-start(bf16[64,2,1024]{2,1,0:T(2,128)(2,1)} %reshape.105), calls=%async_computation | async-start | bytes 524288 | tf_op jit(solution)/shard_map/all_to_all | solution.py:29
  42.2 4.9 copy-start.3
  181.1 17.9 %all-to-all-start.1 = ((bf16[64,2,1024]{2,1,0:T(2,128)(2,1)}), bf16[64,2,1024]{2,1,0:T(2,128)(2,1)}, u32[]{:S(2)}, u32[]{:S(2)}) async-start(bf16[64,2,1024]{2,1,0:T(2,128)(2,1)} %reshape.107), calls=%async_computation.1 | async-start | bytes 524288 | tf_op jit(solution)/shard_map/all_to_all | solution.py:48
  204.5 4.9 copy-start.2
  216.6 24.0 %all-to-all-start.2 = ((bf16[64,2,1024]{2,1,0:T(2,128)(2,1)}), bf16[64,2,1024]{2,1,0:T(2,128)(2,1)S(1)}, u32[]{:S(2)}, u32[]{:S(2)}) async-start(bf16[64,2,1024]{2,1,0:T(2,128)(2,1)} %reshape.109), calls=%async_computation.2 | async-start | bytes 524288 | tf_op jit(solution)/shard_map/all_to_all | solution.py:29
  240.7 161.6 %all-to-all-start.6 = ((bf16[64,2,1024]{2,1,0:T(2,128)(2,1)}), bf16[64,2,1024]{2,1,0:T(2,128)(2,1)}, u32[]{:S(2)}, u32[]{:S(2)}) async-start(bf16[64,2,1024]{2,1,0:T(2,128)(2,1)} %reshape.117), calls=%async_computation.6 | async-start | bytes 524288 | tf_op jit(solution)/shard_map/all_to_all | solution.py:39
  402.3 31.3 %all-to-all-start.3 = ((bf16[64,2,1024]{2,1,0:T(2,128)(2,1)}), bf16[64,2,1024]{2,1,0:T(2,128)(2,1)S(1)}, u32[]{:S(2)}, u32[]{:S(2)}) async-start(bf16[64,2,1024]{2,1,0:T(2,128)(2,1)} %reshape.111), calls=%async_computation.3 | async-start | bytes 524288 | tf_op jit(solution)/shard_map/all_to_all | solution.py:48
  426.7 17.6 %copy-start.8 = (bf16[8,16,1024]{2,1,0:T(8,128)(2,1)S(1)}, bf16[8,16,1024]{2,1,0:T(8,128)(2,1)}, u32[]{:S(2)}) copy-start(bf16[8,16,1024]{2,1,0:T(8,128)(2,1)} %param.9) | copy-start | bytes 786436
  433.5 30.8 %all-to-all-start.7 = ((bf16[64,2,1024]{2,1,0:T(2,128)(2,1)}), bf16[64,2,1024]{2,1,0:T(2,128)(2,1)S(1)}, u32[]{:S(2)}, u32[]{:S(2)}) async-start(bf16[64,2,1024]{2,1,0:T(2,128)(2,1)} %reshape.119), calls=%async_computation.7 | async-start | bytes 524288 | tf_op jit(solution)/shard_map/all_to_all | solution.py:39
  464.3 26.2 %all-to-all-start.4 = ((bf16[64,2,1024]{2,1,0:T(2,128)(2,1)}), bf16[64,2,1024]{2,1,0:T(2,128)(2,1)S(1)}, u32[]{:S(2)}, u32[]{:S(2)}) async-start(bf16[64,2,1024]{2,1,0:T(2,128)(2,1)} %reshape.113), calls=%async_computation.4 | async-start | bytes 524288 | tf_op jit(solution)/shard_map/all_to_all | solution.py:29
  494.7 4.9 copy-start.4
  632.2 11.7 %copy-start.5 = (bf16[1024,1024]{0,1:T(8,128)(2,1)S(1)}, bf16[1024,1024]{0,1:T(8,128)(2,1)}, u32[]{:S(2)}) copy-start(bf16[1024,1024]{0,1:T(8,128)(2,1)} %copy.51) | copy-start | bytes 6291460
  639.1 16.8 %all-to-all-start.8 = ((bf16[64,2,1024]{2,1,0:T(2,128)(2,1)}), bf16[64,2,1024]{2,1,0:T(2,128)(2,1)S(1)}, u32[]{:S(2)}, u32[]{:S(2)}) async-start(bf16[64,2,1024]{2,1,0:T(2,128)(2,1)} %reshape.121), calls=%async_computation.8 | async-start | bytes 524288 | tf_op jit(solution)/shard_map/all_to_all | solution.py:39
  643.9 308.4 %all-reduce.5.cloned.1.call-start = ((), (), s32[]{:S(2)}) async-start(), calls=%async_computation.9 | async-start | bytes 16777216
  660.0 4.9 copy-start.6
  671.3 1.0 copy-start.7
  677.0 19.5 %all-to-all-start.5 = ((bf16[64,2,1024]{2,1,0:T(2,128)(2,1)}), bf16[64,2,1024]{2,1,0:T(2,128)(2,1)S(1)}, u32[]{:S(2)}, u32[]{:S(2)}) async-start(bf16[64,2,1024]{2,1,0:T(2,128)(2,1)} %reshape.115), calls=%async_computation.5 | async-start | bytes 524288 | tf_op jit(solution)/shard_map/all_to_all | solution.py:48
  697.9 257.1 %copy-start.1 = (bf16[512,1024]{1,0:T(8,128)(2,1)S(1)}, bf16[512,1024]{1,0:T(8,128)(2,1)}, u32[]{:S(2)}) copy-start(bf16[512,1024]{1,0:T(8,128)(2,1)} %param.13) | copy-start | bytes 3145732
Sparse Core Ops, SparseCore 0:
  671.4 280.8 all-reduce.4
where the time goes:
time: 971 us; the launch traced here: 962 us
  blocking collectives  383 us (39%)
  waiting for transfers between devices  283 us (29%)
  local copies, waits for them, and re-layouts  164 us (17%)
  starting transfers between devices  72.2 us (7%)
  matrix products  41.4 us (4%)
  between operations  14.7 us (2%)
    psum x3, blocking collectives, on_device(): total = lax.psum(jnp.sum(scaled, axis=(1, 2)), 'state')  383 us
    unnamed x2, waiting for transfers between devices  246 us
    unnamed x42, local copies, waits for them, and re-layouts  62.4 us
    all_to_all x3, starting transfers between devices, on_device(): lax.all_to_all(mixed, 'state', split_axis=2, concat_axis=1, tiled=True)  29 us
    all_to_all x3, starting transfers between devices, on_device(): lax.all_to_all(pulled, 'state', split_axis=1, concat_axis=2, tiled=True)  26.1 us
    all_to_all x6, local copies, waits for them, and re-layouts, on_device(): lax.all_to_all(pulled, 'state', split_axis=1, concat_axis=2, tiled=True)  24.6 us
    all_to_all x6, local copies, waits for them, and re-layouts, on_device(): lax.all_to_all(fresh, 'state', split_axis=1, concat_axis=2, tiled=True)  24.6 us
    all_to_all x6, local copies, waits for them, and re-layouts, on_device(): lax.all_to_all(mixed, 'state', split_axis=2, concat_axis=1, tiled=True)  24.1 us
  transfers between devices with their start and end apart: 10, of which 5 were waited for; matrix products, arithmetic and copies ran while one was open for 11% of the time, Pallas kernels for 0%

commit v1 on v0

--- a/solution.py
+++ b/solution.py
@@ -45,7 +45,12 @@
         )
         loglik = loglik + jnp.log(norm)
         fresh = (scaled / norm[:, None, None]).astype(jnp.bfloat16)
-        alpha = lax.all_to_all(fresh, "state", split_axis=1, concat_axis=2, tiled=True)
+        alpha = jnp.concatenate(
+            lax.all_to_all(
+                jnp.stack(jnp.split(fresh, lax.axis_size("state"), axis=1)), "state", 0, 0
+            ),
+            axis=2,
+        )
     factor = 1.0 / (seq_dev * lax.axis_size("dp") * STEPS)
     terms_rows = trans_rows.astype(f32) * sums_rows * factor
     terms_cols = trans_cols.astype(f32) * sums_cols * factor

time: 971 us -> 1090 us (1.12)
  local copies, waits for them, and re-layouts: 164 us -> 294 us
  waiting for transfers between devices: 283 us -> 265 us
    unnamed x42 -> x229, local copies, waits for them, and re-layouts: 62.4 us -> 188 us
    reshape x0 -> x6, local copies, waits for them, and re-layouts: none -> 24.6 us  [on_device(): jnp.concatenate(lax.all_to_all(jnp.stack(jnp.split(fresh, lax.axis_size('...]
    all_to_all x6 -> x0, local copies, waits for them, and re-layouts: 24.6 us -> none  [on_device(): lax.all_to_all(fresh, 'state', split_axis=1, concat_axis=2, tiled=True)]
    another operation x0 -> x6, local copies, waits for them, and re-layouts: none -> 12.7 us  [on_device(): jnp.stack(jnp.split(fresh, lax.axis_size('state'), axis=1))]
    unnamed x2, waiting for transfers between devices: 246 us -> 234 us
  transfers between devices with their start and end apart: 10 -> 10, of which waited for: 5 -> 4; matrix products, arithmetic and copies ran while one was open for 11% -> 19% of each run, Pallas kernels for 0% -> 0%
where the time goes in v1:
time: 1090 us; the launch traced here: 1080 us
  blocking collectives  384 us (35%)
  local copies, waits for them, and re-layouts  294 us (27%)
  waiting for transfers between devices  265 us (24%)
  starting transfers between devices  76.3 us (7%)
  matrix products  42 us (4%)
  between operations  15 us (1%)
    psum x3, blocking collectives, on_device(): total = lax.psum(jnp.sum(scaled, axis=(1, 2)), 'state')  384 us
    unnamed x2, waiting for transfers between devices  234 us
    unnamed x229, local copies, waits for them, and re-layouts  188 us
    all_to_all x3, starting transfers between devices, on_device(): lax.all_to_all(mixed, 'state', split_axis=2, concat_axis=1, tiled=True)  29 us
    all_to_all x3, starting transfers between devices, on_device(): lax.all_to_all(pulled, 'state', split_axis=1, concat_axis=2, tiled=True)  26.2 us
    all_to_all x6, local copies, waits for them, and re-layouts, on_device(): lax.all_to_all(pulled, 'state', split_axis=1, concat_axis=2, tiled=True)  24.6 us
    reshape x6, local copies, waits for them, and re-layouts, on_device(): jnp.concatenate(lax.all_to_all(jnp.stack(jnp.split(fresh, lax.axis_size('...  24.6 us
    all_to_all x6, local copies, waits for them, and re-layouts, on_device(): lax.all_to_all(mixed, 'state', split_axis=2, concat_axis=1, tiled=True)  24.1 us
  transfers between devices with their start and end apart: 10, of which 4 were waited for; matrix products, arithmetic and copies ran while one was open for 19% of the time, Pallas kernels for 0%

profile of v1, /device:TPU:2, one launch (start us, length us, event | category | flops | bytes accessed | tf_op | source)
XLA Modules:
  0.0 1079.9 jit_solution(16945910652649583743)
XLA Ops:
  14.0 12.1 %all-to-all-start = ((bf16[64,2,1024]{2,1,0:T(2,128)(2,1)}), bf16[64,2,1024]{2,1,0:T(2,128)(2,1)S(1)}, u32[]{:S(2)}, u32[]{:S(2)}) async-start(bf16[64,2,1024]{2,1,0:T(2,128)(2,1)} %reshape.129), calls=%async_computation | async-start | bytes 524288 | tf_op jit(solution)/shard_map/all_to_all | solution.py:29
  28.8 9.3 all-to-all-done
  42.2 4.8 all_to_all.90
  48.3 125.5 %psum.21 = f32[8]{0:T(128)S(1)} all-reduce(f32[8]{0:T(128)S(1)} %get-tuple-element.19), channel_id=1, replica_groups=mesh['dp'=4,'state'=64] {'state'}, use_global_device_ids=true, to_apply=%region_1.3 | all-reduce | flops 8 | bytes 64 | tf_op jit(solution)/shard_map/psum | solution.py:33
  224.5 5.7 all-to-all-start.1
  233.4 8.6 all-to-all-done.1
  247.5 4.8 reshape.47
  259.7 6.0 all-to-all-start.2
  283.7 10.3 all-to-all-start.6
  308.3 129.0 %psum.22 = f32[8]{0:T(128)S(1)} all-reduce(f32[8]{0:T(128)S(1)} %get-tuple-element.21), channel_id=1, replica_groups=mesh['dp'=4,'state'=64] {'state'}, use_global_device_ids=true, to_apply=%region_3.5 | all-reduce | flops 8 | bytes 64 | tf_op jit(solution)/shard_map/psum | solution.py:33
  490.2 4.9 all-to-all-start.3
  505.6 5.3 all_to_all.105
  520.3 10.9 %all-to-all-start.7 = ((bf16[64,2,1024]{2,1,0:T(2,128)(2,1)}), bf16[64,2,1024]{2,1,0:T(2,128)(2,1)S(1)}, u32[]{:S(2)}, u32[]{:S(2)}) async-start(bf16[64,2,1024]{2,1,0:T(2,128)(2,1)} %reshape.143), calls=%async_computation.7 | async-start | bytes 524288 | tf_op jit(solution)/shard_map/all_to_all | solution.py:39
  551.3 10.9 %all-to-all-start.4 = ((bf16[64,2,1024]{2,1,0:T(2,128)(2,1)}), bf16[64,2,1024]{2,1,0:T(2,128)(2,1)}, u32[]{:S(2)}, u32[]{:S(2)}) async-start(bf16[64,2,1024]{2,1,0:T(2,128)(2,1)} %reshape.137), calls=%async_computation.4 | async-start | bytes 524288 | tf_op jit(solution)/shard_map/all_to_all | solution.py:29
  583.0 4.8 all_to_all.100
  589.1 129.1 %psum.23 = f32[8]{0:T(128)S(1)} all-reduce(f32[8]{0:T(128)S(1)} %get-tuple-element.23), channel_id=1, replica_groups=mesh['dp'=4,'state'=64] {'state'}, use_global_device_ids=true, to_apply=%region_5.7 | all-reduce | flops 8 | bytes 64 | tf_op jit(solution)/shard_map/psum | solution.py:33
  725.1 5.0 all-to-all-start.8
  763.1 6.5 fusion.4
  773.7 4.8 all_to_all.113
  778.6 6.4 fusion.2
  802.9 10.6 all-to-all-start.5
  813.5 13.1 %all-to-all-done.5 = bf16[64,2,1024]{2,1,0:T(2,128)(2,1)S(1)} async-done(((bf16[64,2,1024]{2,1,0:T(2,128)(2,1)}), bf16[64,2,1024]{2,1,0:T(2,128)(2,1)S(1)}, u32[]{:S(2)}, u32[]{:S(2)}) %all-to-all-start.5) | async-done | bytes 262176 | tf_op jit(solution)/shard_map/all_to_all | solution.py:49
  830.7 5.4 reshape.51
  836.1 233.8 %all-reduce.5.cloned.1.call-done = (f32[1024,1024]{0,1:T(8,128)}, f32[1024,1024]{0,1:T(8,128)}) async-done(((f32[1024,1024]{0,1:T(8,128)}, f32[1024,1024]{0,1:T(8,128)}), (f32[1024,1024]{0,1:T(8,128)}, f32[1024,1024]{0,1:T(8,128)})) %all-reduce.5.cloned.1.call-update) | async-done | bytes 8388624
  (295 shorter events, 297.3 us)
Async XLA Ops:
  7.2 20.9 %copy-start = (bf16[512,1024]{1,0:T(8,128)(2,1)S(1)}, bf16[512,1024]{1,0:T(8,128)(2,1)}, u32[]{:S(2)}) copy-start(bf16[512,1024]{1,0:T(8,128)(2,1)} %param.13) | copy-start | bytes 3145732
  9.4 16.7 %copy-start.8 = (s32[8,3]{0,1:T(4,128)S(1)}, s32[8,3]{0,1:T(4,128)}, u32[]{:S(2)}) copy-start(s32[8,3]{0,1:T(4,128)} %param.10) | copy-start | bytes 292
  14.0 24.1 %all-to-all-start = ((bf16[64,2,1024]{2,1,0:T(2,128)(2,1)}), bf16[64,2,1024]{2,1,0:T(2,128)(2,1)S(1)}, u32[]{:S(2)}, u32[]{:S(2)}) async-start(bf16[64,2,1024]{2,1,0:T(2,128)(2,1)} %reshape.129), calls=%async_computation | async-start | bytes 524288 | tf_op jit(solution)/shard_map/all_to_all | solution.py:29
  42.2 4.9 copy-start.3
  224.5 17.5 %all-to-all-start.1 = ((bf16[64,2,1024]{2,1,0:T(2,128)(2,1)}), bf16[64,2,1024]{2,1,0:T(2,128)(2,1)}, u32[]{:S(2)}, u32[]{:S(2)}) async-start(bf16[64,2,1024]{2,1,0:T(2,128)(2,1)} %reshape.131), calls=%async_computation.1 | async-start | bytes 524288 | tf_op jit(solution)/shard_map/all_to_all | solution.py:49
  247.5 4.9 copy-start.2
  259.7 24.0 %all-to-all-start.2 = ((bf16[64,2,1024]{2,1,0:T(2,128)(2,1)}), bf16[64,2,1024]{2,1,0:T(2,128)(2,1)S(1)}, u32[]{:S(2)}, u32[]{:S(2)}) async-start(bf16[64,2,1024]{2,1,0:T(2,128)(2,1)} %reshape.133), calls=%async_computation.2 | async-start | bytes 524288 | tf_op jit(solution)/shard_map/all_to_all | solution.py:29
  283.7 206.5 %all-to-all-start.6 = ((bf16[64,2,1024]{2,1,0:T(2,128)(2,1)}), bf16[64,2,1024]{2,1,0:T(2,128)(2,1)S(1)}, u32[]{:S(2)}, u32[]{:S(2)}) async-start(bf16[64,2,1024]{2,1,0:T(2,128)(2,1)} %reshape.141), calls=%async_computation.6 | async-start | bytes 524288 | tf_op jit(solution)/shard_map/all_to_all | solution.py:39
  490.2 30.1 %all-to-all-start.3 = ((bf16[64,2,1024]{2,1,0:T(2,128)(2,1)}), bf16[64,2,1024]{2,1,0:T(2,128)(2,1)S(1)}, u32[]{:S(2)}, u32[]{:S(2)}) async-start(bf16[64,2,1024]{2,1,0:T(2,128)(2,1)} %reshape.135), calls=%async_computation.3 | async-start | bytes 524288 | tf_op jit(solution)/shard_map/all_to_all | solution.py:49
  513.5 17.8 %copy-start.7 = (bf16[8,16,1024]{2,1,0:T(8,128)(2,1)S(1)}, bf16[8,16,1024]{2,1,0:T(8,128)(2,1)}, u32[]{:S(2)}) copy-start(bf16[8,16,1024]{2,1,0:T(8,128)(2,1)} %param.9) | copy-start | bytes 786436
  520.3 31.0 %all-to-all-start.7 = ((bf16[64,2,1024]{2,1,0:T(2,128)(2,1)}), bf16[64,2,1024]{2,1,0:T(2,128)(2,1)S(1)}, u32[]{:S(2)}, u32[]{:S(2)}) async-start(bf16[64,2,1024]{2,1,0:T(2,128)(2,1)} %reshape.143), calls=%async_computation.7 | async-start | bytes 524288 | tf_op jit(solution)/shard_map/all_to_all | solution.py:39
  551.3 26.2 %all-to-all-start.4 = ((bf16[64,2,1024]{2,1,0:T(2,128)(2,1)}), bf16[64,2,1024]{2,1,0:T(2,128)(2,1)}, u32[]{:S(2)}, u32[]{:S(2)}) async-start(bf16[64,2,1024]{2,1,0:T(2,128)(2,1)} %reshape.137), calls=%async_computation.4 | async-start | bytes 524288 | tf_op jit(solution)/shard_map/all_to_all | solution.py:29
  583.0 4.9 copy-start.4
  725.1 38.0 %copy-start.5 = (bf16[1024,1024]{0,1:T(8,128)(2,1)S(1)}, bf16[1024,1024]{0,1:T(8,128)(2,1)}, u32[]{:S(2)}) copy-start(bf16[1024,1024]{0,1:T(8,128)(2,1)} %copy.478) | copy-start | bytes 6291460
  725.1 44.5 %all-to-all-start.8 = ((bf16[64,2,1024]{2,1,0:T(2,128)(2,1)}), bf16[64,2,1024]{2,1,0:T(2,128)(2,1)S(1)}, u32[]{:S(2)}, u32[]{:S(2)}) async-start(bf16[64,2,1024]{2,1,0:T(2,128)(2,1)} %reshape.145), calls=%async_computation.8 | async-start | bytes 524288 | tf_op jit(solution)/shard_map/all_to_all | solution.py:39
  730.0 339.9 %all-reduce.5.cloned.1.call-start = ((), (), s32[]{:S(2)}) async-start(), calls=%async_computation.9 | async-start | bytes 16777216
  773.7 4.9 copy-start.6
  802.9 23.7 %all-to-all-start.5 = ((bf16[64,2,1024]{2,1,0:T(2,128)(2,1)}), bf16[64,2,1024]{2,1,0:T(2,128)(2,1)S(1)}, u32[]{:S(2)}, u32[]{:S(2)}) async-start(bf16[64,2,1024]{2,1,0:T(2,128)(2,1)} %reshape.139), calls=%async_computation.5 | async-start | bytes 524288 | tf_op jit(solution)/shard_map/all_to_all | solution.py:49
  828.0 244.6 %copy-start.1 = (bf16[512,1024]{1,0:T(8,128)(2,1)S(1)}, bf16[512,1024]{1,0:T(8,128)(2,1)}, u32[]{:S(2)}) copy-start(bf16[512,1024]{1,0:T(8,128)(2,1)} %param.13) | copy-start | bytes 3145732
Sparse Core Ops, SparseCore 0:
  785.2 284.7 all-reduce.4
